TPU v7x, 32 devices: a whole 2x2x4 slice. The times are simulated.
32 devices in a mesh: grp: 2 (over y), tm: 4 (over z), height: 2 (over core), head: 2 (over x).
Axes of the slice: x: 2, y: 2, z: 4, core: 2. Of those that a mesh axis runs over, the one named last changes fastest.
Arguments:
- query_video: bfloat16 [32, 16, 16, 3072], P('grp', 'height', 'tm', 'head'), parts along dimension 0, may hold values from -20 to 20
- key_video: bfloat16 [32, 16, 16, 3072], P('grp', 'height', 'tm', 'head'), parts along dimension 0, may hold values from -20 to 20
- value_video: bfloat16 [32, 16, 16, 3072], P('grp', 'height', 'tm', 'head'), parts along dimension 0, may hold values from -6 to 6
- query_text: bfloat16 [512, 3072], P('grp', 'head'), parts along dimension 0, may hold values from -20 to 20
- key_text: bfloat16 [512, 3072], P('grp', 'head'), parts along dimension 0, may hold values from -6 to 6
- value_text: bfloat16 [512, 3072], P('grp', 'head'), parts along dimension 0, may hold values from -6 to 6
- text_valid: int32 [512], P('grp'), parts along dimension 0, may hold values from 0 to 1, as said below
Outputs:
- out_video: bfloat16 [32, 16, 16, 3072], P('grp', 'height', 'tm', 'head'), parts along dimension 0
- out_text: bfloat16 [512, 3072], P('grp', 'head'), parts along dimension 0
There are 2 independent parts, one for each index of `grp`. A program takes and returns all parts, laid end to end along the dimension named above; each array names one. Nothing has to cross between parts.
Inputs may be any that keep to these rules, and one draw needn't show every extreme that they name: `text_valid`: 1 on a leading run of at least 64 positions and 0 on the rest; at least one position is 0.
All inputs are finite; a program needn't handle non-finite values.
Results may differ from a plain program's by a relative error of at most 0.0037.
Values may be sent and summed in bfloat16 or wider, within the bound.
No kernel may reach another device: no remote copies, remote signals or barrier semaphores. Data moves between devices by JAX's collectives and lax.ppermute only.
A program may use at most 192 MiB of HBM per device.

v0:
```python
import math
import jax
import jax.numpy as jnp
from jax import lax
from jax.sharding import PartitionSpec as P

HD = 128
TILE = 4


def with_halo(array, sides, width):
    for axis, dim in sides:
        devices, length = (lax.axis_size(axis), array.shape[dim])
        up = [(i, (i + 1) % devices) for i in range(devices - 1)]
        down = [(j, i) for i, j in up]
        last = lax.slice_in_dim(array, length - width, length, axis=dim)
        initial = lax.slice_in_dim(array, 0, width, axis=dim)
        before = lax.ppermute(last, axis, up)
        after = lax.ppermute(initial, axis, down)
        array = jnp.concatenate([before, array, after], axis=dim)
    return array


def into_tiles(field):
    time_tiles = field.shape[0] // TILE
    row_tiles = field.shape[1] // TILE
    col_tiles = field.shape[2] // TILE
    shaped = field.reshape(time_tiles, TILE, row_tiles, TILE, col_tiles, TILE, field.shape[3])
    shaped = shaped.transpose(0, 2, 4, 1, 3, 5, 6)
    return shaped.reshape(time_tiles, row_tiles, col_tiles, TILE**3, field.shape[3])


def from_tiles(tiles, time_tiles, row_tiles, col_tiles):
    shaped = tiles.reshape(time_tiles, row_tiles, col_tiles, TILE, TILE, TILE, tiles.shape[2])
    shaped = shaped.transpose(0, 3, 1, 4, 2, 5, 6)
    return shaped.reshape(time_tiles * TILE, row_tiles * TILE, col_tiles * TILE, tiles.shape[2])


def shards(query_video, key_video, value_video, query_text, key_text, value_text, text_valid):
    frames = query_video.shape[0]
    features = query_video.shape[3]
    head_count = features // HD
    time_tiles = frames // TILE
    row_tiles = query_video.shape[1] // TILE
    col_tiles = query_video.shape[2] // TILE
    tile_count = time_tiles * row_tiles * col_tiles
    volume = TILE**3
    text_count = query_text.shape[0]
    scale_factor = 1.0 / math.sqrt(HD)
    stacked = jnp.concatenate([key_video, value_video], axis=3)
    padded = with_halo(stacked, (("tm", 2), ("height", 1)), TILE)
    padded = jnp.pad(padded, ((TILE, TILE), (0, 0), (0, 0), (0, 0)))
    grid_shape = (time_tiles + 2, row_tiles + 2, col_tiles + 2, volume, head_count, HD)
    key_grid = into_tiles(padded[:, :, :, :features]).reshape(grid_shape)
    value_grid = into_tiles(padded[:, :, :, features:]).reshape(grid_shape)
    query_tiles = into_tiles(query_video).reshape(tile_count, volume, head_count, HD)
    slot_list = jnp.arange(27, dtype=jnp.int32)
    slot_ids = slot_list[None, :]
    numbering = jnp.arange(tile_count, dtype=jnp.int32)
    tile_time = numbering // (row_tiles * col_tiles)
    tile_row = numbering // col_tiles % row_tiles
    tile_col = numbering % col_tiles
    target_time = tile_time[:, None] + slot_ids // 9 - 1
    target_row = tile_row[:, None] + slot_ids // 3 % 3 - 1
    target_col = tile_col[:, None] + slot_ids % 3 - 1
    global_row = lax.axis_index("height") * row_tiles + target_row
    global_col = lax.axis_index("tm") * col_tiles + target_col
    inside = (target_time >= 0) & (target_time < time_tiles)
    inside = inside & (global_row >= 0) & (global_row < row_tiles * lax.axis_size("height"))
    inside = inside & (global_col >= 0) & (global_col < col_tiles * lax.axis_size("tm"))

    def window_block(grid, slot):
        zero = jnp.zeros((), jnp.int32)
        starts = (slot // 9, slot // 3 % 3, slot % 3, zero, zero, zero)
        block = lax.dynamic_slice(
            grid, starts, (time_tiles, row_tiles, col_tiles, volume, head_count, HD)
        )
        return block.reshape(tile_count, volume, head_count, HD)

    text_keys = key_text.reshape(text_count, head_count, HD)
    text_values = value_text.reshape(text_count, head_count, HD)
    text_queries = query_text.reshape(text_count, head_count, HD)
    text_open = text_valid > 0
    cross_scores = (
        jnp.einsum("qahd,khd->qhak", query_tiles, text_keys, preferred_element_type=jnp.float32)
        * scale_factor
    )
    cross_scores = jnp.where(text_open[None, None, None, :], cross_scores, -jnp.inf)

    def slot_scores(slot, allowed):
        picked = window_block(key_grid, slot)
        scores = (
            jnp.einsum("qahd,qbhd->qhab", query_tiles, picked, preferred_element_type=jnp.float32)
            * scale_factor
        )
        return jnp.where(allowed[:, None, None, None], scores, -jnp.inf)

    def peak_slot(peak, operands):
        scores = slot_scores(operands[0], operands[1])
        return (jnp.maximum(peak, jnp.max(scores, axis=3)), None)

    row_peak, unused = lax.scan(peak_slot, jnp.max(cross_scores, axis=3), (slot_list, inside.T))
    cross_probs = jnp.exp(cross_scores - row_peak[..., None])
    cross_weights = cross_probs.astype(jnp.bfloat16)
    text_part = jnp.einsum(
        "qhak,khd->qahd", cross_weights, text_values, preferred_element_type=jnp.float32
    )

    def add_slot(carry, operands):
        running, total = carry
        slot, allowed = operands
        probs = jnp.exp(slot_scores(slot, allowed) - row_peak[..., None])
        picked = window_block(value_grid, slot)
        running = running + jnp.einsum(
            "qhab,qbhd->qahd",
            probs.astype(jnp.bfloat16),
            picked,
            preferred_element_type=jnp.float32,
        )
        total = total + jnp.sum(probs, axis=3)
        return ((running, total), None)

    (summed, video_total), unused = lax.scan(
        add_slot, (text_part, jnp.sum(cross_probs, axis=3)), (slot_list, inside.T)
    )
    video_out = (summed / video_total.transpose(0, 2, 1)[..., None]).astype(jnp.bfloat16)
    out_video = from_tiles(
        video_out.reshape(tile_count, volume, features), time_tiles, row_tiles, col_tiles
    )
    flat_keys = key_video.reshape(-1, head_count, HD)
    flat_values = value_video.reshape(-1, head_count, HD)
    far_scores = (
        jnp.einsum("khd,nhd->hkn", text_queries, flat_keys, preferred_element_type=jnp.float32)
        * scale_factor
    )
    near_scores = (
        jnp.einsum("khd,jhd->hkj", text_queries, text_keys, preferred_element_type=jnp.float32)
        * scale_factor
    )
    near_scores = jnp.where(text_open[None, None, :], near_scores, -jnp.inf)
    far_peak = lax.pmax(jnp.max(far_scores, axis=2), ("tm", "height"))
    text_peak = jnp.maximum(far_peak, jnp.max(near_scores, axis=2))
    far_probs = jnp.exp(far_scores - text_peak[:, :, None])
    near_probs = jnp.exp(near_scores - text_peak[:, :, None])
    far_total = jnp.sum(far_probs, axis=2).T
    near_total = jnp.sum(near_probs, axis=2).T
    far_summed = jnp.einsum(
        "hkn,nhd->khd",
        far_probs.astype(jnp.bfloat16),
        flat_values,
        preferred_element_type=jnp.float32,
    )
    near_summed = jnp.einsum(
        "hkj,jhd->khd",
        near_probs.astype(jnp.bfloat16),
        text_values,
        preferred_element_type=jnp.float32,
    )
    whole_summed, whole_total = lax.psum((far_summed, far_total), ("tm", "height"))
    finished = (whole_summed + near_summed) / (whole_total + near_total)[:, :, None]
    out_text = finished.astype(jnp.bfloat16).reshape(text_count, features)
    return (out_video, out_text)


def solution(mesh):
    placed = (
        P("grp", "height", "tm", "head"),
        P("grp", "height", "tm", "head"),
        P("grp", "height", "tm", "head"),
        P("grp", "head"),
        P("grp", "head"),
        P("grp", "head"),
        P("grp"),
    )
    return jax.shard_map(
        shards,
        mesh=mesh,
        in_specs=placed,
        out_specs=(P("grp", "height", "tm", "head"), P("grp", "head")),
        check_vma=False,
    )
```

profile of v0, /device:TPU:0, one launch (start us, length us, event | category | flops | bytes accessed | tf_op | source)
XLA Modules:
  0.0 906.2 jit_solution(6479953430431862503)
XLA Ops:
  10.2 5.1 collective-permute-start
  16.7 65.8 %collective-permute-done = bf16[16,8,4,3072]{3,2,1,0:T(4,128)(2,1)S(1)} collective-permute-done((bf16[16,8,4,3072]{3,2,1,0:T(4,128)(2,1)S(1)}, bf16[16,8,4,3072]{3,2,1,0:T(4,128)(2,1)S(1)}, u32[]{:S(2)}, u32[]{:S(2)}) %collective-permute-start) | collective-permute-done | bytes 3145760 | tf_op jit(solution)/shard_map/ppermute | solution.py:18
  82.5 4.3 collective-permute-done.1
  88.5 7.0 pad_maximum_fusion
  95.6 5.1 fusion.69
  118.8 5.9 multiply_reduce_fusion
  124.7 31.5 %pmax.7 = f32[12,256]{1,0:T(8,128)S(1)} all-reduce(f32[12,256]{1,0:T(8,128)S(1)} %get-tuple-element.360), channel_id=1, replica_groups=mesh['grp'=2,'tm'=4,'height'=2,'head'=2] {'tm','height'}, use_global_device_ids=true, to_apply=%region_9.10 | all-reduce | flops 3072 | bytes 24576 | tf_op jit(solution)/shard_map/pmax | solution.py:141
  160.2 5.7 fusion.44
  186.1 26.5 %psum.15 = f32[256,12]{0,1:T(8,128)S(1)} all-reduce(f32[256,12]{0,1:T(8,128)S(1)} %bitcast.156), channel_id=1, replica_groups=mesh['grp'=2,'tm'=4,'height'=2,'head'=2] {'tm','height'}, use_global_device_ids=true, to_apply=%region_13.14 | all-reduce | flops 3072 | bytes 24576 | tf_op jit(solution)/shard_map/psum | solution.py:159
  215.3 10.6 %all-reduce.3.cloned.1.call-done = f32[256,12,128]{2,0,1:T(8,128)} async-done(((f32[256,12,128]{2,0,1:T(8,128)}), f32[256,12,128]{2,0,1:T(8,128)}) %all-reduce.3.cloned.1.call-update) | async-done | bytes 1572880 | tf_op jit(solution)/shard_map/psum | solution.py:159
  226.0 4.8 fusion.36
  235.3 46.5 %select_maximum_fusion = bf16[24,16,12,3072]{3,2,1,0:T(8,128)(2,1)} fusion(bf16[16,4,12,3072]{3,2,1,0:T(8,128)(2,1)} %collective-permute-done.3, bf16[16,4,12,3072]{3,2,1,0:T(8,128)(2,1)} %collective-permute-done.2, bf16[16,8,4,3072]{3,2,1,0:T(4,128)(2,1)} %copy-done.4, bf16[16,8,4,3072]{3,2,1,0:T(4,128)(2,1)S(1)} %constant_dynamic-update-slice_fusion, ...), kind=kLoop, calls=%fused_computation.19 | loop fusion | flops 254803968 | bytes 47185920 | tf_op jit(solution)/shard_map/concatenate | solution.py:20
  281.9 26.4 %fusion.68 = (bf16[24,16,12,1536]{3,2,1,0:T(8,128)(2,1)}, bf16[24,16,12,1536]{3,2,1,0:T(8,128)(2,1)}) fusion(bf16[24,16,12,3072]{3,2,1,0:T(8,128)(2,1)} %select_maximum_fusion), kind=kLoop, calls=%fused_computation.106 | loop fusion | bytes 56623104 | tf_op jit(solution)/shard_map/slice | solution.py:55
  308.2 26.3 %reshape.181 = bf16[6,4,4,4,3,4,1536]{6,5,4,3,2,1,0:T(4,128)(2,1)} reshape(bf16[24,16,12,1536]{3,2,1,0:T(8,128)(2,1)} %get-tuple-element.357) | data formatting | bytes 28311552 | tf_op jit(solution)/shard_map/reshape | solution.py:28
  334.5 12.7 %copy.130 = bf16[6,4,4,4,3,4,1536]{6,5,3,1,4,2,0:T(4,128)(2,1)} copy(bf16[6,4,4,4,3,4,1536]{6,5,4,3,2,1,0:T(4,128)(2,1)} %reshape.181) | data formatting | bytes 28311552 | tf_op jit(solution)/shard_map/reshape | solution.py:28
  347.3 28.4 %reshape_reshape.13 = bf16[6,4,3,64,12,128]{5,4,3,2,1,0:T(8,128)(2,1)} reshape(bf16[6,4,3,4,4,4,1536]{6,5,4,3,2,1,0:T(4,128)(2,1)} %bitcast.134) | data formatting | bytes 28311552 | tf_op jit(solution)/shard_map/reshape;reshape | solution.py:54
  375.6 15.6 %copy.85 = bf16[6,4,3,64,12,128]{5,3,4,1,0,2:T(8,128)(2,1)} copy(bf16[6,4,3,64,12,128]{5,4,3,2,1,0:T(8,128)(2,1)} %reshape_reshape.13) | data formatting | bytes 28311552 | tf_op jit(solution)/shard_map/while | solution.py:102
  391.3 172.4 %while.28 = (s32[]{:T(128)}, f32[8,12,64]{2,1,0:T(8,128)S(1)}, pred[27,8]{1,0:T(8,128)(4,1)S(1)}, s32[27]{0:T(128)S(1)}, bf16[6,4,3,64,12,128]{5,3,4,1,0,2:T(8,1...) while((s32[]{:T(128)}, f32[8,12,64]{2,1,0:T(8,128)S(1)}, ...), condition=%wide.region_3.4_spmd, body=%wide.region_1.3_spmd.sunk | while | flops 101842976 | bytes 6390297 | solution.py:102
  563.7 4.8 fusion.15
  570.2 26.3 %reshape.183 = bf16[6,4,4,4,3,4,1536]{6,5,4,3,2,1,0:T(4,128)(2,1)} reshape(bf16[24,16,12,1536]{3,2,1,0:T(8,128)(2,1)} %get-tuple-element.356) | data formatting | bytes 28311552 | tf_op jit(solution)/shard_map/reshape | solution.py:28
  596.5 12.7 %copy.129 = bf16[6,4,4,4,3,4,1536]{6,5,3,1,4,2,0:T(4,128)(2,1)} copy(bf16[6,4,4,4,3,4,1536]{6,5,4,3,2,1,0:T(4,128)(2,1)} %reshape.183) | data formatting | bytes 28311552 | tf_op jit(solution)/shard_map/reshape | solution.py:28
  609.2 28.4 %reshape_reshape.14 = bf16[6,4,3,64,12,128]{5,4,3,2,1,0:T(8,128)(2,1)} reshape(bf16[6,4,3,4,4,4,1536]{6,5,4,3,2,1,0:T(4,128)(2,1)} %bitcast.135) | data formatting | bytes 28311552 | tf_op jit(solution)/shard_map/reshape;reshape | solution.py:55
  637.6 15.6 %copy.93 = bf16[6,4,3,64,12,128]{5,3,4,1,0,2:T(8,128)(2,1)} copy(bf16[6,4,3,64,12,128]{5,4,3,2,1,0:T(8,128)(2,1)} %reshape_reshape.14) | data formatting | bytes 28311552 | tf_op jit(solution)/shard_map/while | solution.py:123
  653.1 239.0 %while.29 = (s32[]{:T(128)}, f32[8,64,12,128]{3,1,2,0:T(8,128)S(1)}, f32[8,12,64]{2,1,0:T(8,128)S(1)}, s32[27]{0:T(128)S(1)}, bf16[6,4,3,64,12,128]{5,3,4,1,0,2:...) while((s32[]{:T(128)}, ...), condition=%wide.region_7.8_spmd, body=%wide.region_5.7_spmd.sunk | while | flops 205258784 | bytes 26886740 | solution.py:123
  (419 shorter events, 309.3 us)
Async XLA Ops:
  7.2 218.8 %all-reduce.3.cloned.1.call-start = ((), (), s32[]{:S(2)}) async-start(), calls=%async_computation | async-start | bytes 3145728 | tf_op jit(solution)/shard_map/psum | solution.py:159
  10.2 72.3 %collective-permute-start = (bf16[16,8,4,3072]{3,2,1,0:T(4,128)(2,1)S(1)}, bf16[16,8,4,3072]{3,2,1,0:T(4,128)(2,1)S(1)}, u32[]{:S(2)}, u32[]{:S(2)}) collective-permute-start(bf16[16,8,4,3072]{3,2,1,0:T(4,128)(2,1)S(1)} %constant_dynamic-update-slice_fusion), channel_id=1, source_target_pairs={{0,4},{4,8},{8,12},{1,5},{5,9},{9,13},{2,6},{6,10},{10,14},{3,7},{... | collective-permute-start | bytes 9437192 | tf_op jit(solution)/shard_map/ppermute | solution.py:18
  15.4 71.5 %collective-permute-start.1 = (bf16[16,8,4,3072]{3,2,1,0:T(4,128)(2,1)S(1)}, bf16[16,8,4,3072]{3,2,1,0:T(4,128)(2,1)S(1)}, u32[]{:S(2)}, u32[]{:S(2)}) collective-permute-start(bf16[16,8,4,3072]{3,2,1,0:T(4,128)(2,1)S(1)} %constant_dynamic-update-slice_fusion), channel_id=1, source_target_pairs={{4,0},{8,4},{12,8},{5,1},{9,5},{13,9},{6,2},{10,6},{14,10},{7,3},{... | collective-permute-start | bytes 9437192 | tf_op jit(solution)/shard_map/ppermute | solution.py:19
  82.5 4.3 copy-start.3
  100.7 134.7 %collective-permute-start.2 = (bf16[16,4,12,3072]{3,2,1,0:T(8,128)(2,1)}, bf16[16,4,12,3072]{3,2,1,0:T(8,128)(2,1)}, u32[]{:S(2)}, u32[]{:S(2)}) collective-permute-start(bf16[16,4,12,3072]{3,2,1,0:T(8,128)(2,1)} %get-tuple-element.358), channel_id=1, source_target_pairs={{0,2},{1,3},{4,6},{5,7},{8,10},{9,11},{12,14},{13,15},{16,18},{17,... | collective-permute-start | bytes 14155784 | tf_op jit(solution)/shard_map/ppermute | solution.py:18
  104.5 130.8 %collective-permute-start.3 = (bf16[16,4,12,3072]{3,2,1,0:T(8,128)(2,1)}, bf16[16,4,12,3072]{3,2,1,0:T(8,128)(2,1)}, u32[]{:S(2)}, u32[]{:S(2)}) collective-permute-start(bf16[16,4,12,3072]{3,2,1,0:T(8,128)(2,1)} %get-tuple-element.359), channel_id=1, source_target_pairs={{2,0},{3,1},{6,4},{7,5},{10,8},{11,9},{14,12},{15,13},{18,16},{19,... | collective-permute-start | bytes 14155784 | tf_op jit(solution)/shard_map/ppermute | solution.py:19
  118.8 37.4 %copy-start.10 = (s32[256]{0:T(256)S(1)}, s32[256]{0:T(256)}, u32[]{:S(2)}) copy-start(s32[256]{0:T(256)} %param.17) | copy-start | bytes 3076
  156.2 4.0 copy-start.5
  173.3 7.2 slice-start
  175.5 5.0 slice-start.1
  177.8 2.8 copy-start
  375.6 15.6 %copy-start.7 = (bf16[8,64,12,128]{3,1,2,0:T(8,128)(2,1)S(1)}, bf16[8,64,12,128]{3,1,2,0:T(8,128)(2,1)}, u32[]{:S(2)}) copy-start(bf16[8,64,12,128]{3,1,2,0:T(8,128)(2,1)} %copy.86) | copy-start | bytes 4718596
  391.3 177.3 %copy-start.9 = (bf16[256,1536]{0,1:T(8,128)(2,1)S(1)}, bf16[256,1536]{0,1:T(8,128)(2,1)}, u32[]{:S(2)}) copy-start(bf16[256,1536]{0,1:T(8,128)(2,1)} %copy.88) | copy-start | bytes 2359300
  563.7 4.8 copy-start.1
  683.1 2.7 copy-start.8
  709.7 2.7 copy-start.8
  718.5 2.7 copy-start.8
  736.2 2.7 copy-start.8
  745.1 2.7 copy-start.8
  762.8 2.7 copy-start.8
  771.6 2.7 copy-start.8
  798.2 2.7 copy-start.8
  824.7 2.7 copy-start.8
  851.3 2.7 copy-start.8
  (20 other events, 52.1 us)
Sparse Core Ops, SparseCore 0:
  166.0 59.9 all-reduce.2
where the time goes:
time: 919 us; the launch traced here: 906 us
  local copies, waits for them, and re-layouts  388 us (42%)
  loops' own time  166 us (18%)
  matrix products  121 us (13%)
  waiting for transfers between devices  80.8 us (9%)
  other arithmetic  65.6 us (7%)
  blocking collectives  57.9 us (6%)
  between operations  14.5 us (2%)
  starting transfers between devices  11.6 us (1%)
    dynamic_slice x54, local copies, waits for them, and re-layouts, window_block(): lax.dynamic_slice(grid, starts, (time_tiles, row_tiles, col_tiles, volume...  114 us
    another operation x1, loops' own time, shards(): lax.scan(peak_slot, jnp.max(cross_scores, axis=3), (slot_list, inside.T))  87.3 us
    reshape x5, local copies, waits for them, and re-layouts, into_tiles(): field.reshape(time_tiles, TILE, row_tiles, TILE, col_tiles, TILE, field.s...  81.3 us
    another operation x1, loops' own time, shards(): lax.scan(add_slot, (text_part, jnp.sum(cross_probs, axis=3)), (slot_list,...  79.1 us
    ppermute x2, waiting for transfers between devices, with_halo(): before = lax.ppermute(last, axis, up)  65.8 us
    concatenate x2, other arithmetic, with_halo(): array = jnp.concatenate([before, array, after], axis=dim)  53.6 us
    dot_general x54, matrix products, slot_scores(): jnp.einsum('qahd,qbhd->qhab', query_tiles, picked, preferred_element_type...  53 us
    dot_general x27, matrix products, add_slot(): jnp.einsum('qhab,qbhd->qahd', probs.astype(jnp.bfloat16), picked, preferr...  44 us
  transfers between devices with their start and end apart: 5, of which 3 were waited for; matrix products, arithmetic and copies ran while one was open for 7% of the time, Pallas kernels for 0%

commit v1 on v0

--- a/solution.py
+++ b/solution.py
@@ -156,7 +156,7 @@
         text_values,
         preferred_element_type=jnp.float32,
     )
-    whole_summed, whole_total = lax.psum((far_summed, far_total), ("tm", "height"))
+    whole_summed, whole_total = lax.psum(lax.psum((far_summed, far_total), "height"), "tm")
     finished = (whole_summed + near_summed) / (whole_total + near_total)[:, :, None]
     out_text = finished.astype(jnp.bfloat16).reshape(text_count, features)
     return (out_video, out_text)

time: 919 us -> 949 us (1.033)
  starting transfers between devices: 11.6 us -> 24.3 us
  loops' own time: 166 us -> 176 us
    psum x1 -> x2, waiting for transfers between devices: 10.6 us -> 33.6 us  [the longest x1 33.6 us: shards(): lax.psum(lax.psum((far_summed, far_total), 'height'), 'tm')]
    another operation x1, loops' own time: 79.1 us -> 96.7 us  [shards(): lax.scan(add_slot, (text_part, jnp.sum(cross_probs, axis=3)), (slot_list,...]
    ppermute x2, waiting for transfers between devices: 65.8 us -> 49.8 us  [with_halo(): before = lax.ppermute(last, axis, up)]
    psum x1 -> x2, starting transfers between devices: 0.04 us -> 11.4 us  [the longest x1 11.3 us: shards(): lax.psum(lax.psum((far_summed, far_total), 'height'), 'tm')]
    psum x1 -> x2, blocking collectives: 26.5 us -> 20.2 us  [the longest x1 16.8 us: shards(): lax.psum(lax.psum((far_summed, far_total), 'height'), 'tm')]
  transfers between devices with their start and end apart: 5 -> 6, of which waited for: 3 -> 3; matrix products, arithmetic and copies ran while one was open for 7% -> 7% of each run, Pallas kernels for 0% -> 0%
where the time goes in v1:
time: 949 us; the launch traced here: 934 us
  local copies, waits for them, and re-layouts  387 us (41%)
  loops' own time  176 us (19%)
  matrix products  122 us (13%)
  waiting for transfers between devices  89.3 us (9%)
  other arithmetic  71.5 us (8%)
  blocking collectives  49.7 us (5%)
  starting transfers between devices  24.3 us (3%)
  between operations  14.7 us (2%)
    dynamic_slice x54, local copies, waits for them, and re-layouts, window_block(): lax.dynamic_slice(grid, starts, (time_tiles, row_tiles, col_tiles, volume...  114 us
    another operation x1, loops' own time, shards(): lax.scan(add_slot, (text_part, jnp.sum(cross_probs, axis=3)), (slot_list,...  96.7 us
    reshape x5, local copies, waits for them, and re-layouts, into_tiles(): field.reshape(time_tiles, TILE, row_tiles, TILE, col_tiles, TILE, field.s...  81.3 us
    another operation x1, loops' own time, shards(): lax.scan(peak_slot, jnp.max(cross_scores, axis=3), (slot_list, inside.T))  79.7 us
    concatenate x2, other arithmetic, with_halo(): array = jnp.concatenate([before, array, after], axis=dim)  54.6 us
    dot_general x54, matrix products, slot_scores(): jnp.einsum('qahd,qbhd->qhab', query_tiles, picked, preferred_element_type...  53 us
    ppermute x2, waiting for transfers between devices, with_halo(): before = lax.ppermute(last, axis, up)  49.8 us
    dot_general x27, matrix products, add_slot(): jnp.einsum('qhab,qbhd->qahd', probs.astype(jnp.bfloat16), picked, preferr...  44 us
  transfers between devices with their start and end apart: 6, of which 3 were waited for; matrix products, arithmetic and copies ran while one was open for 7% of the time, Pallas kernels for 0%

profile of v1, /device:TPU:0, one launch (start us, length us, event | category | flops | bytes accessed | tf_op | source)
XLA Modules:
  0.0 934.2 jit_solution(8284217873482483861)
XLA Ops:
  10.2 6.5 collective-permute-start
  26.8 5.9 multiply_reduce_fusion
  32.7 49.8 %collective-permute-done = bf16[16,8,4,3072]{3,2,1,0:T(4,128)(2,1)} collective-permute-done((bf16[16,8,4,3072]{3,2,1,0:T(4,128)(2,1)S(1)}, bf16[16,8,4,3072]{3,2,1,0:T(4,128)(2,1)}, u32[]{:S(2)}, u32[]{:S(2)}) %collective-permute-start) | collective-permute-done | bytes 3145760 | tf_op jit(solution)/shard_map/ppermute | solution.py:18
  82.5 5.8 collective-permute-done.1
  88.3 8.1 pad_maximum_fusion
  96.4 5.2 fusion.69
  113.5 29.5 %pmax.7 = f32[12,256]{1,0:T(8,128)S(1)} all-reduce(f32[12,256]{1,0:T(8,128)S(1)} %get-tuple-element.360), channel_id=1, replica_groups=mesh['grp'=2,'tm'=4,'height'=2,'head'=2] {'tm','height'}, use_global_device_ids=true, to_apply=%region_9.10 | all-reduce | flops 3072 | bytes 24576 | tf_op jit(solution)/shard_map/pmax | solution.py:141
  143.0 6.3 fusion.44
  149.3 11.3 %all-reduce.6.cloned.1.call-start = ((), (), s32[]{:S(2)}) async-start(), calls=%async_computation.1 | async-start | bytes 3145728 | tf_op jit(solution)/shard_map/psum | solution.py:159
  188.7 16.8 %psum.31 = f32[256,12]{0,1:T(8,128)S(1)} all-reduce(f32[256,12]{0,1:T(8,128)S(1)} %psum.30), channel_id=1, replica_groups=mesh['grp'=2,'tm'=4,'height'=2,'head'=2] {'tm'}, use_global_device_ids=true, to_apply=%region_15.16 | all-reduce | flops 3072 | bytes 24576 | tf_op jit(solution)/shard_map/psum | solution.py:159
  208.3 33.6 %all-reduce.6.cloned.1.call-done = f32[256,12,128]{2,0,1:T(8,128)} async-done(((f32[256,12,128]{2,0,1:T(8,128)}), f32[256,12,128]{2,0,1:T(8,128)}) %all-reduce.6.cloned.1.call-update) | async-done | bytes 1572880 | tf_op jit(solution)/shard_map/psum | solution.py:159
  242.0 4.8 fusion.36
  251.4 46.6 %select_maximum_fusion = bf16[24,16,12,3072]{3,2,1,0:T(8,128)(2,1)} fusion(bf16[16,4,12,3072]{3,2,1,0:T(8,128)(2,1)} %collective-permute-done.3, bf16[16,4,12,3072]{3,2,1,0:T(8,128)(2,1)} %collective-permute-done.2, bf16[16,8,4,3072]{3,2,1,0:T(4,128)(2,1)} %collective-permute-done.1, bf16[16,8,4,3072]{3,2,1,0:T(4,128)(2,1)S(1)} %constant_dynamic-update-slice_fusion, ...), kind=kLoop, calls=%fused_computation.19 | loop fusion | flops 254803968 | bytes 47185920 | tf_op jit(solution)/shard_map/concatenate | solution.py:20
  297.9 26.2 %fusion.68 = (bf16[24,16,12,1536]{3,2,1,0:T(8,128)(2,1)}, bf16[24,16,12,1536]{3,2,1,0:T(8,128)(2,1)}) fusion(bf16[24,16,12,3072]{3,2,1,0:T(8,128)(2,1)} %select_maximum_fusion), kind=kLoop, calls=%fused_computation.106 | loop fusion | bytes 56623104 | tf_op jit(solution)/shard_map/slice | solution.py:55
  324.2 26.3 %reshape.181 = bf16[6,4,4,4,3,4,1536]{6,5,4,3,2,1,0:T(4,128)(2,1)} reshape(bf16[24,16,12,1536]{3,2,1,0:T(8,128)(2,1)} %get-tuple-element.357) | data formatting | bytes 28311552 | tf_op jit(solution)/shard_map/reshape | solution.py:28
  350.4 12.7 %copy.130 = bf16[6,4,4,4,3,4,1536]{6,5,3,1,4,2,0:T(4,128)(2,1)} copy(bf16[6,4,4,4,3,4,1536]{6,5,4,3,2,1,0:T(4,128)(2,1)} %reshape.181) | data formatting | bytes 28311552 | tf_op jit(solution)/shard_map/reshape | solution.py:28
  363.2 28.4 %reshape_reshape.13 = bf16[6,4,3,64,12,128]{5,4,3,2,1,0:T(8,128)(2,1)} reshape(bf16[6,4,3,4,4,4,1536]{6,5,4,3,2,1,0:T(4,128)(2,1)} %bitcast.134) | data formatting | bytes 28311552 | tf_op jit(solution)/shard_map/reshape;reshape | solution.py:54
  391.6 15.7 %copy.85 = bf16[6,4,3,64,12,128]{5,3,4,1,0,2:T(8,128)(2,1)} copy(bf16[6,4,3,64,12,128]{5,4,3,2,1,0:T(8,128)(2,1)} %reshape_reshape.13) | data formatting | bytes 28311552 | tf_op jit(solution)/shard_map/while | solution.py:102
  407.2 164.3 %while.28 = (s32[]{:T(128)}, f32[8,12,64]{2,1,0:T(8,128)S(1)}, pred[27,8]{1,0:T(8,128)(4,1)S(1)}, s32[27]{0:T(128)S(1)}, bf16[6,4,3,64,12,128]{5,3,4,1,0,2:T(8,1...) while((s32[]{:T(128)}, f32[8,12,64]{2,1,0:T(8,128)S(1)}, ...), condition=%wide.region_3.4_spmd, body=%wide.region_1.3_spmd.sunk | while | flops 101842976 | bytes 6390297 | solution.py:102
  578.0 26.3 %reshape.183 = bf16[6,4,4,4,3,4,1536]{6,5,4,3,2,1,0:T(4,128)(2,1)} reshape(bf16[24,16,12,1536]{3,2,1,0:T(8,128)(2,1)} %get-tuple-element.356) | data formatting | bytes 28311552 | tf_op jit(solution)/shard_map/reshape | solution.py:28
  604.3 12.7 %copy.129 = bf16[6,4,4,4,3,4,1536]{6,5,3,1,4,2,0:T(4,128)(2,1)} copy(bf16[6,4,4,4,3,4,1536]{6,5,4,3,2,1,0:T(4,128)(2,1)} %reshape.183) | data formatting | bytes 28311552 | tf_op jit(solution)/shard_map/reshape | solution.py:28
  617.0 28.4 %reshape_reshape.14 = bf16[6,4,3,64,12,128]{5,4,3,2,1,0:T(8,128)(2,1)} reshape(bf16[6,4,3,4,4,4,1536]{6,5,4,3,2,1,0:T(4,128)(2,1)} %bitcast.135) | data formatting | bytes 28311552 | tf_op jit(solution)/shard_map/reshape;reshape | solution.py:55
  645.4 15.5 %copy.93 = bf16[6,4,3,64,12,128]{5,3,4,1,0,2:T(8,128)(2,1)} copy(bf16[6,4,3,64,12,128]{5,4,3,2,1,0:T(8,128)(2,1)} %reshape_reshape.14) | data formatting | bytes 28311552 | tf_op jit(solution)/shard_map/while | solution.py:123
  660.9 259.0 %while.29 = (s32[]{:T(128)}, f32[8,64,12,128]{3,1,2,0:T(8,128)S(1)}, f32[8,12,64]{2,1,0:T(8,128)S(1)}, s32[27]{0:T(128)S(1)}, bf16[6,4,3,64,12,128]{5,3,4,1,0,2:...) while((s32[]{:T(128)}, ...), condition=%wide.region_7.8_spmd, body=%wide.region_5.7_spmd.sunk | while | flops 205258784 | bytes 26886740 | solution.py:123
  (416 shorter events, 320.6 us)
Async XLA Ops:
  7.2 166.8 %all-reduce.4.cloned.1.call-start = ((), (), s32[]{:S(2)}) async-start(), calls=%async_computation | async-start | bytes 3145728 | tf_op jit(solution)/shard_map/psum | solution.py:159
  10.2 16.6 %copy-start.9 = (s32[256]{0:T(256)S(1)}, s32[256]{0:T(256)}, u32[]{:S(2)}) copy-start(s32[256]{0:T(256)} %param.17) | copy-start | bytes 3076
  10.2 72.3 %collective-permute-start = (bf16[16,8,4,3072]{3,2,1,0:T(4,128)(2,1)S(1)}, bf16[16,8,4,3072]{3,2,1,0:T(4,128)(2,1)}, u32[]{:S(2)}, u32[]{:S(2)}) collective-permute-start(bf16[16,8,4,3072]{3,2,1,0:T(4,128)(2,1)S(1)} %constant_dynamic-update-slice_fusion), channel_id=1, source_target_pairs={{0,4},{4,8},{8,12},{1,5},{5,9},{9,13},{2,6},{6,10},{10,14},{3,7},{... | collective-permute-start | bytes 9437192 | tf_op jit(solution)/shard_map/ppermute | solution.py:18
  16.8 71.5 %collective-permute-start.1 = (bf16[16,8,4,3072]{3,2,1,0:T(4,128)(2,1)S(1)}, bf16[16,8,4,3072]{3,2,1,0:T(4,128)(2,1)}, u32[]{:S(2)}, u32[]{:S(2)}) collective-permute-start(bf16[16,8,4,3072]{3,2,1,0:T(4,128)(2,1)S(1)} %constant_dynamic-update-slice_fusion), channel_id=1, source_target_pairs={{4,0},{8,4},{12,8},{5,1},{9,5},{13,9},{6,2},{10,6},{14,10},{7,3},{... | collective-permute-start | bytes 9437192 | tf_op jit(solution)/shard_map/ppermute | solution.py:19
  96.4 10.4 %copy-start.2 = (bf16[256,1536]{0,1:T(8,128)(2,1)S(1)}, bf16[256,1536]{0,1:T(8,128)(2,1)}, u32[]{:S(2)}) copy-start(bf16[256,1536]{0,1:T(8,128)(2,1)} %copy.79) | copy-start | bytes 2359300
  96.4 10.4 %copy-start.4 = (bf16[256,1536]{0,1:T(8,128)(2,1)S(1)}, bf16[256,1536]{0,1:T(8,128)(2,1)}, u32[]{:S(2)}) copy-start(bf16[256,1536]{0,1:T(8,128)(2,1)} %copy.98) | copy-start | bytes 2359300
  101.7 149.7 %collective-permute-start.2 = (bf16[16,4,12,3072]{3,2,1,0:T(8,128)(2,1)}, bf16[16,4,12,3072]{3,2,1,0:T(8,128)(2,1)}, u32[]{:S(2)}, u32[]{:S(2)}) collective-permute-start(bf16[16,4,12,3072]{3,2,1,0:T(8,128)(2,1)} %get-tuple-element.358), channel_id=1, source_target_pairs={{0,2},{1,3},{4,6},{5,7},{8,10},{9,11},{12,14},{13,15},{16,18},{17,... | collective-permute-start | bytes 14155784 | tf_op jit(solution)/shard_map/ppermute | solution.py:18
  105.5 145.8 %collective-permute-start.3 = (bf16[16,4,12,3072]{3,2,1,0:T(8,128)(2,1)}, bf16[16,4,12,3072]{3,2,1,0:T(8,128)(2,1)}, u32[]{:S(2)}, u32[]{:S(2)}) collective-permute-start(bf16[16,4,12,3072]{3,2,1,0:T(8,128)(2,1)} %get-tuple-element.359), channel_id=1, source_target_pairs={{2,0},{3,1},{6,4},{7,5},{10,8},{11,9},{14,12},{15,13},{18,16},{19,... | collective-permute-start | bytes 14155784 | tf_op jit(solution)/shard_map/ppermute | solution.py:19
  149.3 92.7 %all-reduce.6.cloned.1.call-start = ((), (), s32[]{:S(2)}) async-start(), calls=%async_computation.1 | async-start | bytes 3145728 | tf_op jit(solution)/shard_map/psum | solution.py:159
  174.0 3.8 copy-start.1
  391.6 15.7 %copy-start.6 = (bf16[8,64,12,128]{3,1,2,0:T(8,128)(2,1)S(1)}, bf16[8,64,12,128]{3,1,2,0:T(8,128)(2,1)}, u32[]{:S(2)}) copy-start(bf16[8,64,12,128]{3,1,2,0:T(8,128)(2,1)} %copy.86) | copy-start | bytes 4718596
  407.2 169.1 %copy-start.8 = (bf16[256,1536]{0,1:T(8,128)(2,1)S(1)}, bf16[256,1536]{0,1:T(8,128)(2,1)}, u32[]{:S(2)}) copy-start(bf16[256,1536]{0,1:T(8,128)(2,1)} %copy.88) | copy-start | bytes 2359300
  571.6 4.8 copy-start
  665.1 2.7 copy-start.7
  674.7 2.7 copy-start.7
  741.8 2.7 copy-start.7
  751.4 2.7 copy-start.7
  761.0 2.7 copy-start.7
  770.6 2.7 copy-start.7
  780.2 2.7 copy-start.7
  789.8 2.7 copy-start.7
  799.4 2.7 copy-start.7
  809.0 2.7 copy-start.7
  914.5 2.7 copy-start.7
  (18 other events, 48.0 us)
Sparse Core Ops, SparseCore 0:
  149.4 18.5 all-reduce.3
  174.1 67.7 all-reduce.5
